TPU v7x, 32 devices: a whole 2x2x4 slice. The times are simulated.
32 devices in a mesh: groups: 2 (over y), patch: 8 (over z, x), req: 2 (over core).
Axes of the slice: x: 2, y: 2, z: 4, core: 2. Of those that a mesh axis runs over, the one named last changes fastest.
Arguments:
- hidden: float32 [16, 8, 64, 1280], P(('groups', 'req'), 'patch'), parts along dimension 0
- skip: float32 [16, 8, 64, 1280], P(('groups', 'req'), 'patch'), parts along dimension 0, may hold values from -6 to 6
- timestep_embedding_table: float32 [50, 1280], replicated, may hold values from -5 to 5
- timesteps: int32 [16], P(('groups', 'req')), parts along dimension 0, may hold values from 0 to 49, as said below
- group_norm_gain: float32 [1280], replicated, may hold values from 0.1 to 1.9
- group_norm_bias: float32 [1280], replicated, may hold values from -3 to 3
- kernel_weight: bfloat16 [9, 1280, 1280], P(None, 'patch', 'req'), may hold values from -0.0546875 to 0.0546875
- adapter_down_weight: bfloat16 [32, 64, 11520], P(('groups', 'patch')), parts along dimension 0, may hold values from -0.0546875 to 0.0546875
- adapter_up_weight: bfloat16 [32, 64, 1280], P(('groups', 'patch')), parts along dimension 0, may hold values from -0.75 to 0.75
- request_adapter: int32 [16], P(('groups', 'req')), parts along dimension 0, may hold values from 0 to 15
- adapter_row_table: int32 [32], P('groups'), parts along dimension 0, may hold values from 0 to 15, each once
Outputs:
- block_out: float32 [16, 8, 64, 1280], P(('groups', 'req'), 'patch'), parts along dimension 0
There are 2 independent parts, one for each index of `groups`. A program takes and returns all parts, laid end to end along the dimension named above; an argument that names none is the same for every part. Nothing has to cross between parts.
Inputs may be any that keep to these rules, and one draw needn't show every extreme that they name: adapter_row_table[a] is the store row of adapter a; every row is used once. Requests 0 and 1 have different timesteps.
All inputs are finite; a program needn't handle non-finite values.
Results may differ from a plain program's by a relative error of at most 0.0026.
Values may be sent and summed in bfloat16 or wider, within the bound.
A program may use at most 128 MiB of HBM per device.

v0:
```python
import jax
import jax.numpy as jnp
from jax import lax
from jax.sharding import PartitionSpec as P

GROUPS = 32


def broadcast(block, axis, owner):
    block = jnp.where(lax.axis_index(axis) == owner, block, jnp.zeros_like(block))
    return lax.psum(block, axis)


def padded(cells, sides, width):
    for axis, dim in sides:
        count = lax.axis_size(axis)
        ends = count - 1
        head = lax.slice_in_dim(cells, 0, width, axis=dim)
        tail = lax.slice_in_dim(cells, cells.shape[dim] - width, cells.shape[dim], axis=dim)
        cells = jnp.concatenate(
            [
                lax.ppermute(tail, axis, [(i, (i + 1) % count) for i in range(ends)]),
                cells,
                lax.ppermute(head, axis, [((i + 1) % count, i) for i in range(ends)]),
            ],
            axis=dim,
        )
    return cells


def from_partner(x, axis, stride):
    return lax.ppermute(x, axis, [(i, i ^ 1 << stride) for i in range(lax.axis_size(axis))])


def make_taps(extended, rows, width):
    pieces = [extended[:, dy : dy + rows, dx : dx + width, :] for dy in range(3) for dx in range(3)]
    stacked = jnp.stack(pieces, axis=3)
    count = stacked.shape[0] * rows * width
    return stacked.reshape(count, 9, stacked.shape[-1])


def load_adapter_factors(
    adapter_down_weight, adapter_up_weight, request_adapter, adapter_row_table, request_total
):
    resident_count = adapter_down_weight.shape[0]
    fetched = []
    for request in range(request_total):
        resident_row = adapter_row_table[request_adapter[request]]
        owner = resident_row // resident_count
        store_position = resident_row % resident_count
        resident_down = lax.dynamic_index_in_dim(
            adapter_down_weight, store_position, 0, keepdims=False
        )
        resident_up = lax.dynamic_index_in_dim(adapter_up_weight, store_position, 0, keepdims=False)
        fetched.append(
            (broadcast(resident_down, "patch", owner), broadcast(resident_up, "patch", owner))
        )
    return fetched


def shards(
    hidden,
    skip,
    timestep_embedding_table,
    timesteps,
    group_norm_gain,
    group_norm_bias,
    kernel_weight,
    adapter_down_weight,
    adapter_up_weight,
    request_adapter,
    adapter_row_table,
):
    request_total, rows, width, chans = hidden.shape
    steps_count = timestep_embedding_table.shape[0]
    onehot = (timesteps[:, None] == jnp.arange(steps_count, dtype=jnp.int32)[None, :]).astype(
        jnp.float32
    )
    temb = jnp.dot(
        onehot,
        timestep_embedding_table,
        preferred_element_type=jnp.float32,
        precision=lax.Precision.HIGHEST,
    )
    shifted = hidden + temb[:, None, None, :]
    grouped = shifted.reshape(request_total, rows, width, GROUPS, chans // GROUPS)
    count = rows * lax.axis_size("patch") * width * (chans // GROUPS)
    totals = lax.psum(jnp.sum(grouped, axis=(1, 2, 4)), "patch")
    mean = totals / count
    centered = grouped - mean[:, None, None, :, None]
    squares = lax.psum(jnp.sum(centered * centered, axis=(1, 2, 4)), "patch")
    var = squares / count
    normed = (centered * lax.rsqrt(var + 1e-05)[:, None, None, :, None]).reshape(
        request_total, rows, width, chans
    )
    act = jax.nn.silu(normed * group_norm_gain + group_norm_bias).astype(jnp.bfloat16)
    extended = padded(act, (("patch", 1),), 1)
    extended = jnp.pad(extended, ((0, 0), (0, 0), (1, 1), (0, 0)))
    partner = from_partner(extended, "req", 0)
    taps = make_taps(jnp.concatenate([extended, partner], axis=0), rows, width)
    pixels = request_total * rows * width
    conv_half = jnp.einsum(
        "ptc,tco->po",
        taps,
        lax.all_gather(kernel_weight, "patch", axis=1, tiled=True),
        preferred_element_type=jnp.float32,
    )
    own_half = conv_half[:pixels]
    returned = from_partner(conv_half[pixels:], "req", 0)
    first = lax.axis_index("req") == 0
    left_half = jnp.where(first, own_half, returned)
    right_half = jnp.where(first, returned, own_half)
    conv = jnp.concatenate([left_half, right_half], axis=1).reshape(
        request_total, rows * width, chans
    )
    own_taps = taps[:pixels].reshape(request_total, rows * width, 9 * chans)
    adapter_factors = load_adapter_factors(
        adapter_down_weight, adapter_up_weight, request_adapter, adapter_row_table, request_total
    )
    deltas = []
    for request in range(request_total):
        down_factor, upper_limit = adapter_factors[request]
        low = lax.dot_general(
            own_taps[request],
            down_factor,
            (((1,), (1,)), ((), ())),
            preferred_element_type=jnp.float32,
        ).astype(jnp.bfloat16)
        deltas.append(jnp.dot(low, upper_limit, preferred_element_type=jnp.float32))
    total = conv + jnp.stack(deltas, axis=0)
    return skip + total.reshape(request_total, rows, width, chans)


def solution(mesh):
    return jax.shard_map(
        shards,
        mesh=mesh,
        in_specs=(
            P(("groups", "req"), "patch", None, None),
            P(("groups", "req"), "patch", None, None),
            P(),
            P(("groups", "req")),
            P(),
            P(),
            P(None, "patch", "req"),
            P(("groups", "patch"), None, None),
            P(("groups", "patch"), None, None),
            P(("groups", "req")),
            P("groups"),
        ),
        out_specs=P(("groups", "req"), "patch", None, None),
        check_vma=False,
    )
```

profile of v0, /device:TPU:1, one launch (start us, length us, event | category | flops | bytes accessed | tf_op | source)
XLA Modules:
  0.0 518.1 jit_solution(13756354301383934993)
XLA Ops:
  6.5 1.5 fusion.27
  15.8 1.5 fusion.26
  27.7 5.8 %select_bitcast_fusion.3 = (bf16[64,11520]{1,0:T(8,128)(2,1)}, bf16[64,11520]{1,0:T(8,128)(2,1)}, bf16[64,11520]{1,0:T(8,128)(2,1)}, bf16[64,11520]{1,0:T(8,128)(2,1)}) fusion(bf16[2,64,11520]{2,1,0:T(8,128)(2,1)} %param.18, s32[]{:T(128)S(6)} %select_n.157, pred[]{:T(512)S(6)} %eq.41, s32[]{:T(128)S(6)} %select_n.167, pred[]{:T(512)S(6)} %eq.42, ...), kind=kLoop, calls=%fused_computation.31 | loop fusion | flops 2949120 | bytes 11796500 | tf_op jit(solution)/shard_map/jit(_where)/select_n | solution.py:10
  36.0 19.5 %psum.70 = f32[4,32]{1,0:T(4,128)S(1)} all-reduce(f32[4,32]{1,0:T(4,128)S(1)} %reduce_sum.25), channel_id=1, replica_groups=mesh['groups'=2,'patch'=8,'req'=2] {'patch'}, use_global_device_ids=true, to_apply=%region_2.0 | all-reduce | flops 128 | bytes 1024 | tf_op jit(solution)/shard_map/psum | solution.py:88
  56.2 15.0 %psum.71 = f32[4,32]{1,0:T(4,128)S(1)} all-reduce(f32[4,32]{1,0:T(4,128)S(1)} %reduce_sum.37), channel_id=1, replica_groups=mesh['groups'=2,'patch'=8,'req'=2] {'patch'}, use_global_device_ids=true, to_apply=%region_5.6 | all-reduce | flops 128 | bytes 1024 | tf_op jit(solution)/shard_map/psum | solution.py:91
  71.9 3.5 collective-permute-start
  75.3 1.5 collective-permute-start.1
  76.8 28.0 %collective-permute-done = bf16[4,1,64,1280]{3,2,1,0:T(8,128)(2,1)S(1)} collective-permute-done((bf16[4,1,64,1280]{3,2,1,0:T(8,128)(2,1)S(1)}, bf16[4,1,64,1280]{3,2,1,0:T(8,128)(2,1)S(1)}, u32[]{:S(2)}, u32[]{:S(2)}) %collective-permute-start) | collective-permute-done | bytes 655392 | tf_op jit(solution)/shard_map/ppermute | solution.py:22
  105.6 4.5 collective-permute-start.2
  110.1 4.1 collective-permute-done.2
  114.2 1.3 bitcast_dynamic-update-slice_fusion.7
  115.4 1.5 bitcast_dynamic-update-slice_fusion.6
  116.9 1.5 bitcast_dynamic-update-slice_fusion.5
  118.4 1.3 bitcast_dynamic-update-slice_fusion.4
  119.7 1.5 bitcast_dynamic-update-slice_fusion.3
  121.2 1.5 bitcast_dynamic-update-slice_fusion.2
  122.6 1.3 bitcast_dynamic-update-slice_fusion.1
  123.9 1.5 bitcast_dynamic-update-slice_fusion
  125.4 1.5 bitcast_dynamic-update-slice_fusion.8
  126.9 4.3 copy-done.3
  131.2 3.1 fusion.25
  134.3 1.2 copy.55
  135.5 1.2 copy.56
  145.1 1.2 constant_dynamic-update-slice_fusion.1
  147.5 128.3 %all-reduce.4.cloned.1.call-done = (bf16[64,1280]{1,0:T(8,128)(2,1)}, bf16[64,11520]{1,0:T(8,128)(2,1)}, bf16[64,1280]{1,0:T(8,128)(2,1)}, bf16[64,11520]{1,0:T(...) async-done(((bf16[64,1280]{1,0:T(8,128)(2,1)}, bf16[64,11520]{1,0:T(8,128)(2,1)}, ...) | async-done | bytes 6553616 | tf_op jit(solution)/shard_map/psum | solution.py:11
  275.8 3.3 convolution_bitcast_fusion.3
  279.1 200.0 %all-gather.2.cloned.1.call-done = bf16[9,1280,640]{2,1,0:T(8,128)(2,1)} async-done(((bf16[9,160,640]{2,1,0:T(8,128)(2,1)}), bf16[9,1280,640]{2,1,0:T(8,128)(2,1)}) %all-gather.2.cloned.1.call-update) | async-done | bytes 14745616 | tf_op jit(solution)/shard_map/all_gather | solution.py:105
  479.1 16.5 %convolution_bitcast_fusion.4 = f32[512,640]{1,0:T(8,128)S(1)} fusion(bf16[512,9,1280]{2,0,1:T(8,128)(2,1)} %constant_dynamic-update-slice_fusion, bf16[9,1280,640]{2,1,0:T(8,128)(2,1)} %all-gather.2.cloned.1.call-done), kind=kOutput, calls=%fused_computation.32 | convolution fusion | flops 7549747200 | bytes 27852800 | tf_op jit(solution)/shard_map/ptc,tco->po/dot_general | solution.py:102
  498.7 3.3 convolution_bitcast_fusion.2
  502.0 2.9 convolution_bitcast_fusion.1
  504.9 2.2 convolution_bitcast_fusion
  509.9 1.3 fusion.14
  (69 shorter events, 19.8 us)
Async XLA Ops:
  6.5 28.6 %copy-start = (f32[50,1280]{1,0:T(8,128)S(1)}, f32[50,1280]{1,0:T(8,128)}, u32[]{:S(2)}) copy-start(f32[50,1280]{1,0:T(8,128)} %param.13) | copy-start | bytes 768004
  6.5 269.2 %all-reduce.4.cloned.1.call-start = ((), (), s32[]{:S(2)}) async-start(), calls=%async_computation.1 | async-start | bytes 13107200 | tf_op jit(solution)/shard_map/psum | solution.py:11
  27.7 5.8 %copy-start.8 = (bf16[2,64,1280]{2,1,0:T(8,128)(2,1)S(1)}, bf16[2,64,1280]{2,1,0:T(8,128)(2,1)}, u32[]{:S(2)}) copy-start(bf16[2,64,1280]{2,1,0:T(8,128)(2,1)} %param.19) | copy-start | bytes 983044
  34.4 0.8 copy-start.16
  34.4 1.3 copy-start.2
  34.4 444.7 %all-gather.2.cloned.1.call-start = ((), (), s32[]{:S(2)}) async-start(), calls=%async_computation | async-start | bytes 16588800 | tf_op jit(solution)/shard_map/all_gather | solution.py:105
  35.7 35.7 %copy-start.14 = (f32[1280]{0:T(1024)S(1)}, f32[1280]{0:T(1024)}, u32[]{:S(2)}) copy-start(f32[1280]{0:T(1024)} %param.16) | copy-start | bytes 15364
  35.7 35.7 %copy-start.15 = (f32[1280]{0:T(1024)S(1)}, f32[1280]{0:T(1024)}, u32[]{:S(2)}) copy-start(f32[1280]{0:T(1024)} %param.15) | copy-start | bytes 15364
  71.9 33.0 %collective-permute-start = (bf16[4,1,64,1280]{3,2,1,0:T(8,128)(2,1)S(1)}, bf16[4,1,64,1280]{3,2,1,0:T(8,128)(2,1)S(1)}, u32[]{:S(2)}, u32[]{:S(2)}) collective-permute-start(bf16[4,1,64,1280]{3,2,1,0:T(8,128)(2,1)S(1)} %multiply_convert_fusion), channel_id=1, source_target_pairs={{0,2},{2,4},{4,6},{6,8},{8,10},{10,12},{12,14},{1,3},{3,5},{5,7},{... | collective-permute-start | bytes 1966088 | tf_op jit(solution)/shard_map/ppermute | solution.py:22
  75.3 29.5 %collective-permute-start.1 = (bf16[4,1,64,1280]{3,2,1,0:T(8,128)(2,1)S(1)}, bf16[4,1,64,1280]{3,2,1,0:T(8,128)(2,1)S(1)}, u32[]{:S(2)}, u32[]{:S(2)}) collective-permute-start(bf16[4,1,64,1280]{3,2,1,0:T(8,128)(2,1)S(1)} %multiply_convert_fusion), channel_id=1, source_target_pairs={{2,0},{4,2},{6,4},{8,6},{10,8},{12,10},{14,12},{3,1},{5,3},{7,5},{... | collective-permute-start | bytes 1966088 | tf_op jit(solution)/shard_map/ppermute | solution.py:24
  105.6 8.5 %collective-permute-start.2 = (bf16[4,3,66,1280]{3,2,1,0:T(8,128)(2,1)S(1)}, bf16[4,3,66,1280]{3,2,1,0:T(8,128)(2,1)}, u32[]{:S(2)}, u32[]{:S(2)}) collective-permute-start(bf16[4,3,66,1280]{3,2,1,0:T(8,128)(2,1)S(1)} %fusion.5), channel_id=1, source_target_pairs={{0,1},{1,0},{2,3},{3,2},{4,5},{5,4},{6,7},{7,6},{8,9},{9,8},{10,11... | collective-permute-start | bytes 6082568 | tf_op jit(solution)/shard_map/ppermute | solution.py:32
  126.9 4.3 copy-start.3
  279.1 219.6 %copy-start.13 = (bf16[64,1280]{1,0:T(8,128)(2,1)S(1)}, bf16[64,1280]{1,0:T(8,128)(2,1)}, u32[]{:S(2)}) copy-start(bf16[64,1280]{1,0:T(8,128)(2,1)} %get-tuple-element.9) | copy-start | bytes 491524
  495.6 1.1 copy-start.9
  497.6 9.6 %collective-permute-start.3 = (f32[256,640]{1,0:T(8,128)}, f32[256,640]{1,0:T(8,128)}, u32[]{:S(2)}, u32[]{:S(2)}) collective-permute-start(f32[256,640]{1,0:T(8,128)} %slice.103), channel_id=1, source_target_pairs={{0,1},{1,0},{2,3},{3,2},{4,5},{5,4},{6,7},{7,6},{8,9},{9,8},{10,11... | collective-permute-start | bytes 1966088 | tf_op jit(solution)/shard_map/ppermute | solution.py:32
  498.7 3.3 copy-start.12
  502.0 2.9 copy-start.11
  504.9 2.3 copy-start.10
  508.4 1.3 copy-start.4
  508.4 1.4 copy-start.5
  508.4 1.4 copy-start.6
  508.4 1.5 copy-start.7
  508.5 2.7 copy-start.1
Sparse Core Ops, SparseCore 0:
  34.5 241.2 all-reduce.3
  278.0 201.0 all-gather.1
where the time goes:
time: 519 us; the launch traced here: 518 us
  waiting for transfers between devices  361 us (70%)
  blocking collectives  34.5 us (7%)
  between operations  31.9 us (6%)
  matrix products  28.6 us (6%)
  local copies, waits for them, and re-layouts  27.8 us (5%)
  other arithmetic  23.6 us (5%)
  starting transfers between devices  10.5 us (2%)
    all_gather x1, waiting for transfers between devices, shards(): lax.all_gather(kernel_weight, 'patch', axis=1, tiled=True)  200 us
    psum x1, waiting for transfers between devices, broadcast(): return lax.psum(block, axis)  128 us
    ppermute x1, waiting for transfers between devices, padded(): lax.ppermute(tail, axis, [(i, (i + 1) % count) for i in range(ends)])  28 us
    psum x1, blocking collectives, shards(): totals = lax.psum(jnp.sum(grouped, axis=(1, 2, 4)), 'patch')  19.5 us
    unnamed x46, local copies, waits for them, and re-layouts  19.1 us
    dot_general x1, matrix products, shards(): jnp.einsum('ptc,tco->po', taps, lax.all_gather(kernel_weight, 'patch', ax...  16.5 us
    psum x1, blocking collectives, shards(): squares = lax.psum(jnp.sum(centered * centered, axis=(1, 2, 4)), 'patch')  15 us
    dot_general x4, matrix products, shards(): deltas.append(jnp.dot(low, upper_limit, preferred_element_type=jnp.float32))  11.8 us
  transfers between devices with their start and end apart: 6, of which 4 were waited for; matrix products, arithmetic and copies ran while one was open for 8% of the time, Pallas kernels for 0%

commit v1 on v0

--- a/solution.py
+++ b/solution.py
@@ -88,7 +88,11 @@
     totals = lax.psum(jnp.sum(grouped, axis=(1, 2, 4)), "patch")
     mean = totals / count
     centered = grouped - mean[:, None, None, :, None]
-    squares = lax.psum(jnp.sum(centered * centered, axis=(1, 2, 4)), "patch")
+
+    def point_the_circles(payload, net_axis):
+        return jax.lax.all_gather(payload, net_axis).sum(axis=0)
+
+    squares = point_the_circles(jnp.sum(centered * centered, axis=(1, 2, 4)), "patch")
     var = squares / count
     normed = (centered * lax.rsqrt(var + 1e-05)[:, None, None, :, None]).reshape(
         request_total, rows, width, chans

time: 519 us -> 519 us (level)
  blocking collectives: 34.5 us -> 43.8 us
  waiting for transfers between devices: 361 us -> 352 us
    all_gather x0 -> x1, blocking collectives: none -> 24.3 us  [point_the_circles(): return jax.lax.all_gather(payload, net_axis).sum(axis=0)]
    psum x1 -> x0, blocking collectives: 15 us -> none  [shards(): squares = lax.psum(jnp.sum(centered * centered, axis=(1, 2, 4)), 'patch')]
    ppermute x1, waiting for transfers between devices: 28 us -> 14.9 us  [padded(): lax.ppermute(tail, axis, [(i, (i + 1) % count) for i in range(ends)])]
where the time goes in v1:
time: 519 us; the launch traced here: 518 us
  waiting for transfers between devices  352 us (68%)
  blocking collectives  43.8 us (8%)
  between operations  31.9 us (6%)
  matrix products  28.6 us (6%)
  local copies, waits for them, and re-layouts  27.8 us (5%)
  other arithmetic  23.7 us (5%)
  starting transfers between devices  9.93 us (2%)
    all_gather x1, waiting for transfers between devices, shards(): lax.all_gather(kernel_weight, 'patch', axis=1, tiled=True)  200 us
    psum x1, waiting for transfers between devices, broadcast(): return lax.psum(block, axis)  132 us
    all_gather x1, blocking collectives, point_the_circles(): return jax.lax.all_gather(payload, net_axis).sum(axis=0)  24.3 us
    psum x1, blocking collectives, shards(): totals = lax.psum(jnp.sum(grouped, axis=(1, 2, 4)), 'patch')  19.5 us
    unnamed x46, local copies, waits for them, and re-layouts  19.1 us
    dot_general x1, matrix products, shards(): jnp.einsum('ptc,tco->po', taps, lax.all_gather(kernel_weight, 'patch', ax...  16.5 us
    ppermute x1, waiting for transfers between devices, padded(): lax.ppermute(tail, axis, [(i, (i + 1) % count) for i in range(ends)])  14.9 us
    dot_general x4, matrix products, shards(): deltas.append(jnp.dot(low, upper_limit, preferred_element_type=jnp.float32))  11.8 us
  transfers between devices with their start and end apart: 6, of which 4 were waited for; matrix products, arithmetic and copies ran while one was open for 8% of the time, Pallas kernels for 0%

profile of v1, /device:TPU:1, one launch (start us, length us, event | category | flops | bytes accessed | tf_op | source)
XLA Modules:
  0.0 517.6 jit_solution(8946679550984637128)
XLA Ops:
  6.5 1.5 fusion.27
  15.8 1.5 fusion.26
  27.7 5.8 %select_bitcast_fusion.3 = (bf16[64,11520]{1,0:T(8,128)(2,1)}, bf16[64,11520]{1,0:T(8,128)(2,1)}, bf16[64,11520]{1,0:T(8,128)(2,1)}, bf16[64,11520]{1,0:T(8,128)(2,1)}) fusion(bf16[2,64,11520]{2,1,0:T(8,128)(2,1)} %param.18, s32[]{:T(128)S(6)} %select_n.157, pred[]{:T(512)S(6)} %eq.41, s32[]{:T(128)S(6)} %select_n.167, pred[]{:T(512)S(6)} %eq.42, ...), kind=kLoop, calls=%fused_computation.31 | loop fusion | flops 2949120 | bytes 11796500 | tf_op jit(solution)/shard_map/jit(_where)/select_n | solution.py:10
  36.0 19.5 %psum.63 = f32[4,32]{1,0:T(4,128)S(1)} all-reduce(f32[4,32]{1,0:T(4,128)S(1)} %reduce_sum.36), channel_id=1, replica_groups=mesh['groups'=2,'patch'=8,'req'=2] {'patch'}, use_global_device_ids=true, to_apply=%region_2.0 | all-reduce | flops 128 | bytes 1024 | tf_op jit(solution)/shard_map/psum | solution.py:88
  56.2 24.3 %all-gather.1 = f32[8,4,32]{2,1,0:T(4,128)S(1)} all-gather(f32[1,4,32]{2,1,0:T(4,128)S(1)} %bitcast.138), channel_id=2, replica_groups=mesh['groups'=2,'patch'=8,'req'=2] {'patch'}, dimensions={0}, use_global_device_ids=true | all-gather | bytes 4608 | tf_op jit(solution)/shard_map/all_gather | solution.py:93
  81.2 1.3 collective-permute-start
  82.5 1.5 collective-permute-start.1
  84.0 14.9 %collective-permute-done = bf16[4,1,64,1280]{3,2,1,0:T(8,128)(2,1)S(1)} collective-permute-done((bf16[4,1,64,1280]{3,2,1,0:T(8,128)(2,1)S(1)}, bf16[4,1,64,1280]{3,2,1,0:T(8,128)(2,1)S(1)}, u32[]{:S(2)}, u32[]{:S(2)}) %collective-permute-start) | collective-permute-done | bytes 655392 | tf_op jit(solution)/shard_map/ppermute | solution.py:22
  99.7 6.0 %collective-permute-start.2 = (bf16[4,3,66,1280]{3,2,1,0:T(8,128)(2,1)S(1)}, bf16[4,3,66,1280]{3,2,1,0:T(8,128)(2,1)}, u32[]{:S(2)}, u32[]{:S(2)}) collective-permute-start(bf16[4,3,66,1280]{3,2,1,0:T(8,128)(2,1)S(1)} %fusion.5), channel_id=1, source_target_pairs={{0,1},{1,0},{2,3},{3,2},{4,5},{5,4},{6,7},{7,6},{8,9},{9,8},{10,11... | collective-permute-start | bytes 6082568 | tf_op jit(solution)/shard_map/ppermute | solution.py:32
  105.7 4.1 collective-permute-done.2
  109.8 1.3 bitcast_dynamic-update-slice_fusion.7
  111.0 1.5 bitcast_dynamic-update-slice_fusion.6
  112.5 1.5 bitcast_dynamic-update-slice_fusion.5
  114.0 1.3 bitcast_dynamic-update-slice_fusion.4
  115.3 1.5 bitcast_dynamic-update-slice_fusion.3
  116.8 1.5 bitcast_dynamic-update-slice_fusion.2
  118.2 1.3 bitcast_dynamic-update-slice_fusion.1
  119.5 1.5 bitcast_dynamic-update-slice_fusion
  121.0 1.5 bitcast_dynamic-update-slice_fusion.8
  122.5 4.3 copy-done.3
  126.8 3.1 fusion.25
  129.9 1.2 copy.68
  131.1 1.2 copy.69
  140.7 1.2 constant_dynamic-update-slice_fusion.1
  143.1 132.2 %all-reduce.4.cloned.1.call-done = (bf16[64,1280]{1,0:T(8,128)(2,1)}, bf16[64,11520]{1,0:T(8,128)(2,1)}, bf16[64,1280]{1,0:T(8,128)(2,1)}, bf16[64,11520]{1,0:T(...) async-done(((bf16[64,1280]{1,0:T(8,128)(2,1)}, bf16[64,11520]{1,0:T(8,128)(2,1)}, ...) | async-done | bytes 6553616 | tf_op jit(solution)/shard_map/psum | solution.py:11
  275.3 3.3 convolution_bitcast_fusion.3
  278.6 200.0 %all-gather.4.cloned.1.call-done = bf16[9,1280,640]{2,1,0:T(8,128)(2,1)} async-done(((bf16[9,160,640]{2,1,0:T(8,128)(2,1)}), bf16[9,1280,640]{2,1,0:T(8,128)(2,1)}) %all-gather.4.cloned.1.call-update) | async-done | bytes 14745616 | tf_op jit(solution)/shard_map/all_gather | solution.py:109
  478.6 16.5 %convolution_bitcast_fusion.4 = f32[512,640]{1,0:T(8,128)S(1)} fusion(bf16[512,9,1280]{2,0,1:T(8,128)(2,1)} %constant_dynamic-update-slice_fusion, bf16[9,1280,640]{2,1,0:T(8,128)(2,1)} %all-gather.4.cloned.1.call-done), kind=kOutput, calls=%fused_computation.32 | convolution fusion | flops 7549747200 | bytes 27852800 | tf_op jit(solution)/shard_map/ptc,tco->po/dot_general | solution.py:106
  498.2 3.3 convolution_bitcast_fusion.2
  501.6 2.9 convolution_bitcast_fusion.1
  504.5 2.2 convolution_bitcast_fusion
  509.5 1.3 fusion.14
  (70 shorter events, 19.8 us)
Async XLA Ops:
  6.5 28.6 %copy-start = (f32[50,1280]{1,0:T(8,128)S(1)}, f32[50,1280]{1,0:T(8,128)}, u32[]{:S(2)}) copy-start(f32[50,1280]{1,0:T(8,128)} %param.13) | copy-start | bytes 768004
  6.5 268.8 %all-reduce.4.cloned.1.call-start = ((), (), s32[]{:S(2)}) async-start(), calls=%async_computation.1 | async-start | bytes 13107200 | tf_op jit(solution)/shard_map/psum | solution.py:11
  27.7 5.8 %copy-start.8 = (bf16[2,64,1280]{2,1,0:T(8,128)(2,1)S(1)}, bf16[2,64,1280]{2,1,0:T(8,128)(2,1)}, u32[]{:S(2)}) copy-start(bf16[2,64,1280]{2,1,0:T(8,128)(2,1)} %param.19) | copy-start | bytes 983044
  34.4 0.8 copy-start.16
  34.4 1.3 copy-start.2
  34.4 444.2 %all-gather.4.cloned.1.call-start = ((), (), s32[]{:S(2)}) async-start(), calls=%async_computation | async-start | bytes 16588800 | tf_op jit(solution)/shard_map/all_gather | solution.py:109
  35.7 45.0 %copy-start.14 = (f32[1280]{0:T(1024)S(1)}, f32[1280]{0:T(1024)}, u32[]{:S(2)}) copy-start(f32[1280]{0:T(1024)} %param.16) | copy-start | bytes 15364
  35.7 45.0 %copy-start.15 = (f32[1280]{0:T(1024)S(1)}, f32[1280]{0:T(1024)}, u32[]{:S(2)}) copy-start(f32[1280]{0:T(1024)} %param.15) | copy-start | bytes 15364
  81.2 17.7 %collective-permute-start = (bf16[4,1,64,1280]{3,2,1,0:T(8,128)(2,1)S(1)}, bf16[4,1,64,1280]{3,2,1,0:T(8,128)(2,1)S(1)}, u32[]{:S(2)}, u32[]{:S(2)}) collective-permute-start(bf16[4,1,64,1280]{3,2,1,0:T(8,128)(2,1)S(1)} %multiply_convert_fusion), channel_id=1, source_target_pairs={{0,2},{2,4},{4,6},{6,8},{8,10},{10,12},{12,14},{1,3},{3,5},{5,7},{... | collective-permute-start | bytes 1966088 | tf_op jit(solution)/shard_map/ppermute | solution.py:22
  82.5 16.4 %collective-permute-start.1 = (bf16[4,1,64,1280]{3,2,1,0:T(8,128)(2,1)S(1)}, bf16[4,1,64,1280]{3,2,1,0:T(8,128)(2,1)S(1)}, u32[]{:S(2)}, u32[]{:S(2)}) collective-permute-start(bf16[4,1,64,1280]{3,2,1,0:T(8,128)(2,1)S(1)} %multiply_convert_fusion), channel_id=1, source_target_pairs={{2,0},{4,2},{6,4},{8,6},{10,8},{12,10},{14,12},{3,1},{5,3},{7,5},{... | collective-permute-start | bytes 1966088 | tf_op jit(solution)/shard_map/ppermute | solution.py:24
  99.7 10.1 %collective-permute-start.2 = (bf16[4,3,66,1280]{3,2,1,0:T(8,128)(2,1)S(1)}, bf16[4,3,66,1280]{3,2,1,0:T(8,128)(2,1)}, u32[]{:S(2)}, u32[]{:S(2)}) collective-permute-start(bf16[4,3,66,1280]{3,2,1,0:T(8,128)(2,1)S(1)} %fusion.5), channel_id=1, source_target_pairs={{0,1},{1,0},{2,3},{3,2},{4,5},{5,4},{6,7},{7,6},{8,9},{9,8},{10,11... | collective-permute-start | bytes 6082568 | tf_op jit(solution)/shard_map/ppermute | solution.py:32
  122.5 4.3 copy-start.3
  278.6 219.6 %copy-start.13 = (bf16[64,1280]{1,0:T(8,128)(2,1)S(1)}, bf16[64,1280]{1,0:T(8,128)(2,1)}, u32[]{:S(2)}) copy-start(bf16[64,1280]{1,0:T(8,128)(2,1)} %get-tuple-element.9) | copy-start | bytes 491524
  495.2 1.1 copy-start.9
  497.1 9.6 %collective-permute-start.3 = (f32[256,640]{1,0:T(8,128)}, f32[256,640]{1,0:T(8,128)}, u32[]{:S(2)}, u32[]{:S(2)}) collective-permute-start(f32[256,640]{1,0:T(8,128)} %slice.103), channel_id=1, source_target_pairs={{0,1},{1,0},{2,3},{3,2},{4,5},{5,4},{6,7},{7,6},{8,9},{9,8},{10,11... | collective-permute-start | bytes 1966088 | tf_op jit(solution)/shard_map/ppermute | solution.py:32
  498.2 3.3 copy-start.12
  501.6 2.9 copy-start.11
  504.5 2.2 copy-start.10
  507.9 1.3 copy-start.4
  507.9 1.4 copy-start.5
  508.0 1.4 copy-start.6
  508.0 1.5 copy-start.7
  508.1 2.7 copy-start.1
Sparse Core Ops, SparseCore 0:
  34.5 240.8 all-reduce.3
  277.5 201.0 all-gather.3
